TPU v7x, 32 devices: a whole 2x2x4 slice. The times are simulated.
32 devices in a mesh: row: 2 (over y), col: 16 (over z, x, core).
Axes of the slice: x: 2, y: 2, z: 4, core: 2. Of those that a mesh axis runs over, the one named last changes fastest.
Arguments:
- velocity: bfloat16 [3, 512, 1024, 256], P(None, 'row', 'col'), may hold values from -6 to 6
- adj_temp: bfloat16 [512, 1024, 256], P('row', 'col'), may hold values from -6 to 6
- radial_div: bfloat16 [256, 256], replicated, may hold values from -0.375 to 0.375
- reciprocal_distance: float32 [256], replicated, may hold values from 0.002 to 0.02
- radial_basis: bfloat16 [168, 256, 256], P('row'), may hold values from -0.375 to 0.375
- radial_eig: float32 [168, 256], P('row'), may hold values from 0.5 to 8
- axial_diff: bfloat16 [1024, 1024], replicated, may hold values from -0.1875 to 0.1875
- axial_basis: bfloat16 [1024, 1024], replicated, may hold values from -0.1875 to 0.1875
- axial_eig: float32 [1024], replicated, may hold values from 0.5 to 8
Outputs:
- new_temp: float32 [168, 2, 1024, 256], P('row', None, 'col')
All inputs are finite; a program needn't handle non-finite values.
Results may differ from a plain program's by a relative error of at most 0.0055.
Values may be sent and summed in bfloat16 or wider, within the bound.
A program may use at most 256 MiB of HBM per device.

v0:
```python
import functools
import math

import jax
import jax.numpy as jnp
from jax import lax
from jax.experimental import pallas as pl
from jax.experimental.pallas import tpu as pltpu
from jax.sharding import PartitionSpec as P


HEAT_OFFSET = 1.0
BF = jnp.bfloat16
F32 = jnp.float32


def wave_rows(first_mode, mode_count, first_angle, angle_count, circle):
    mode_ids = first_mode + jnp.arange(mode_count, dtype=jnp.int32)
    angle_ids = first_angle + jnp.arange(angle_count, dtype=jnp.int32)
    phase_index = mode_ids[:, None] * angle_ids[None, :] % circle
    angle_value = phase_index.astype(F32) * (2.0 * math.pi / circle)
    norm_factor = 1.0 / math.sqrt(circle)
    table = jnp.stack(
        [jnp.cos(angle_value) * norm_factor, -jnp.sin(angle_value) * norm_factor], axis=1
    )
    return table.astype(BF)


def chunk_count(modes):
    return max(c for c in range(1, 5) if modes % c == 0)


def round_up(value, unit):
    return -(-value // unit) * unit


def sums_kernel(modes, padded, vel_ref, adj_ref, div_ref, table_ref, scale_ref, *refs):
    *out_refs, field_s, sum_s = refs
    angles, block, radial = adj_ref.shape
    adj = adj_ref[...].astype(F32)
    for f in range(3):
        flux = (vel_ref[f].astype(F32) * adj).astype(BF)
        if f == 0:
            moved = lax.dot_general(
                flux.reshape(angles * block, radial),
                div_ref[...],
                (((1,), (1,)), ((), ())),
                preferred_element_type=F32,
            ).reshape(angles, block, radial)
            flux = (HEAT_OFFSET * adj + moved).astype(BF)
        field_s[f] = jnp.swapaxes(flux, 0, 1)

    def one(z, carry):
        heat, turn, flux = (
            jnp.dot(table_ref[...], field_s[f, z], preferred_element_type=F32) for f in range(3)
        )
        scale = scale_ref[...]
        sum_s[0, z] = heat[:padded] - scale * turn[padded:]
        sum_s[1, z] = flux[:padded]
        sum_s[2, z] = heat[padded:] + scale * turn[:padded]
        sum_s[3, z] = flux[padded:]
        return carry

    lax.fori_loop(0, block, one, 0)
    for k in range(4):
        turned = jnp.swapaxes(sum_s[k], 0, 1)
        step = modes // len(out_refs)
        for c, out_ref in enumerate(out_refs):
            out_ref[:, k // 2, k % 2] = turned[c * step : (c + 1) * step].astype(BF)


def azimuth_sums(velocity, adj_temp, radial_div, table, mode_values, reciprocal_distance, parts):
    modes = table.shape[0]
    angles, own_axial, radial = adj_temp.shape
    padded = round_up(modes, 8)
    block = 16 if own_axial % 16 == 0 else own_axial
    table = jnp.pad(jnp.moveaxis(table, 1, 0), ((0, 0), (0, padded - modes), (0, 0)))
    table = table.reshape(2 * padded, angles)
    scale = jnp.pad(
        mode_values[:, None] * reciprocal_distance[None], ((0, padded - modes), (0, 0))
    )
    flops = 2 * own_axial * radial * angles * (radial + 6 * padded)
    return pl.pallas_call(
        functools.partial(sums_kernel, modes, padded),
        grid=(own_axial // block,),
        in_specs=[
            pl.BlockSpec((3, angles, block, radial), lambda z: (0, 0, z, 0)),
            pl.BlockSpec((angles, block, radial), lambda z: (0, z, 0)),
            pl.BlockSpec((radial, radial), lambda z: (0, 0)),
            pl.BlockSpec((2 * padded, angles), lambda z: (0, 0)),
            pl.BlockSpec((padded, radial), lambda z: (0, 0)),
        ],
        out_specs=[
            pl.BlockSpec((modes // parts, 2, 2, block, radial), lambda z: (0, 0, 0, z, 0))
        ]
        * parts,
        out_shape=[jax.ShapeDtypeStruct((modes // parts, 2, 2, own_axial, radial), BF)] * parts,
        scratch_shapes=[
            pltpu.VMEM((3, block, angles, radial), BF),
            pltpu.VMEM((4, block, padded, radial), F32),
        ],
        compiler_params=pltpu.CompilerParams(vmem_limit_bytes=60 * 2**20),
        cost_estimate=pl.CostEstimate(
            flops=flops, bytes_accessed=8 * angles * own_axial * radial, transcendentals=0
        ),
        name="sums",
    )(velocity, adj_temp, radial_div, table, scale)


def radial_kernel(count, *refs):
    own_ref, others, basis_ref, out_ref = refs[0], refs[1:-2], refs[-2], refs[-1]
    radial = basis_ref.shape[1]
    for m in range(count):
        total = own_ref[m].astype(F32)
        for other in others:
            total = total + other[m].astype(F32)
        width = total.shape[0] * total.shape[1] * total.shape[2]
        hat = lax.dot_general(
            basis_ref[m],
            total.astype(BF).reshape(width, radial),
            (((0,), (1,)), ((), ())),
            preferred_element_type=F32,
        ).astype(BF)
        out_ref[:, m] = hat.reshape(out_ref.shape[0], out_ref.shape[2], width)


def radial_forward(own, others, basis, first, step, col_total):
    radial = basis.shape[1]
    width = 4 * own.shape[3]
    count = max(c for c in range(1, 8) if step % c == 0)
    skip = first // count
    field = (count, 2, 2, own.shape[3], radial)
    return pl.pallas_call(
        functools.partial(radial_kernel, count),
        grid=(step // count,),
        in_specs=[pl.BlockSpec(field, lambda m: (m, 0, 0, 0, 0)) for _ in (own, *others)]
        + [pl.BlockSpec((count, radial, radial), lambda m: (m + skip, 0, 0))],
        out_specs=pl.BlockSpec(
            (col_total, count, radial // col_total, width), lambda m: (0, m, 0, 0)
        ),
        out_shape=jax.ShapeDtypeStruct((col_total, step, radial // col_total, width), BF),
        compiler_params=pltpu.CompilerParams(vmem_limit_bytes=60 * 2**20),
        cost_estimate=pl.CostEstimate(
            flops=2 * step * radial * radial * width,
            bytes_accessed=2 * step * radial * (radial + 3 * width),
            transcendentals=0,
        ),
        name="radial",
    )(own, *others, basis)


def axial_kernel(lines_ref, forward_ref, basis_ref, radial_ref, axial_ref, out_ref):
    col_total, count, own_count, width = lines_ref.shape
    half = width // 2
    quarter = width // 4
    rows = count * own_count
    lines = jnp.concatenate(
        [
            jnp.concatenate(
                [
                    lines_ref[s, :, :, p * half : (p + 1) * half].reshape(rows, half)
                    for s in range(col_total)
                ],
                axis=1,
            )
            for p in range(2)
        ],
        axis=0,
    )
    coefficients = jnp.dot(lines, forward_ref[...], preferred_element_type=F32)
    eigen = radial_ref[...] + axial_ref[...] + HEAT_OFFSET
    coefficients = jnp.concatenate([coefficients[:rows] / eigen, coefficients[rows:] / eigen], axis=0)
    returned = lax.dot_general(
        coefficients.astype(BF),
        basis_ref[...],
        (((1,), (1,)), ((), ())),
        preferred_element_type=F32,
    )
    for s in range(col_total):
        own = slice(s * quarter, (s + 1) * quarter)
        pair = jnp.concatenate([returned[:rows, own], returned[rows:, own]], axis=1)
        out_ref[s] = pair.astype(BF).reshape(count, own_count, half)


def axial_solve(lines, forward, axial_basis, radial_values, axial_eig):
    col_total, step, own_count, width = lines.shape
    points = axial_basis.shape[0]
    count = max(c for c in range(1, 8) if step % c == 0)
    rows = step * own_count
    return pl.pallas_call(
        axial_kernel,
        grid=(step // count,),
        in_specs=[
            pl.BlockSpec((col_total, count, own_count, width), lambda m: (0, m, 0, 0)),
            pl.BlockSpec((2 * points, points), lambda m: (0, 0)),
            pl.BlockSpec((points, points), lambda m: (0, 0)),
            pl.BlockSpec((count * own_count, 1), lambda m: (m, 0)),
            pl.BlockSpec((1, points), lambda m: (0, 0)),
        ],
        out_specs=pl.BlockSpec((col_total, count, own_count, width // 2), lambda m: (0, m, 0, 0)),
        out_shape=jax.ShapeDtypeStruct((col_total, step, own_count, width // 2), BF),
        compiler_params=pltpu.CompilerParams(vmem_limit_bytes=60 * 2**20),
        cost_estimate=pl.CostEstimate(
            flops=12 * rows * points * points,
            bytes_accessed=6 * points * points + 6 * rows * points,
            transcendentals=0,
        ),
        name="axial",
    )(lines, forward, axial_basis, radial_values.reshape(rows, 1), axial_eig.reshape(1, points))


def last_kernel(count, returned_ref, basis_ref, *refs):
    out_ref = refs[-1]
    for m in range(count):
        lines = returned_ref[:, m]
        lines = lines.reshape(lines.shape[0] * lines.shape[1], lines.shape[2])
        out_ref[m] = lax.dot_general(
            lines, basis_ref[m], (((0,), (1,)), ((), ())), preferred_element_type=F32
        ).reshape(out_ref.shape[1:])


def radial_back(returned, basis, before, first):
    col_total, step, own_count, width = returned.shape
    modes, radial, _ = basis.shape
    count = max(c for c in range(1, 8) if step % c == 0)
    skip = first // count
    return pl.pallas_call(
        functools.partial(last_kernel, count),
        grid=(step // count,),
        in_specs=[
            pl.BlockSpec((col_total, count, own_count, width), lambda m: (0, m, 0, 0)),
            pl.BlockSpec((count, radial, radial), lambda m: (m + skip, 0, 0)),
        ]
        + [pl.BlockSpec(memory_space=pl.ANY) for _ in before],
        out_specs=pl.BlockSpec((count, 2, width // 2, radial), lambda m: (m + skip, 0, 0, 0)),
        out_shape=jax.ShapeDtypeStruct((modes, 2, width // 2, radial), F32),
        input_output_aliases={2: 0} if before else {},
        compiler_params=pltpu.CompilerParams(vmem_limit_bytes=60 * 2**20),
        cost_estimate=pl.CostEstimate(
            flops=2 * step * radial * radial * width,
            bytes_accessed=2 * step * radial * (radial + 3 * width),
            transcendentals=0,
        ),
        name="last",
    )(returned, basis, *before)


def body(
    velocity,
    adj_temp,
    radial_div,
    reciprocal_distance,
    radial_basis,
    radial_eig,
    axial_diff,
    axial_basis,
    axial_eig,
):
    row_total = lax.axis_size("row")
    col_total = lax.axis_size("col")
    row_place = lax.axis_index("row")
    col_place = lax.axis_index("col")
    modes = radial_basis.shape[0]
    angles, own_axial, radial_points = adj_temp.shape
    axial_points = axial_basis.shape[0]
    own_count = radial_points // col_total
    circle = angles * row_total
    parts = chunk_count(modes)
    step = modes // parts

    def partial_sums(place):
        table = wave_rows(place * modes, modes, row_place * angles, angles, circle)
        mode_values = (place * modes + jnp.arange(modes, dtype=jnp.int32)).astype(F32)
        return azimuth_sums(
            velocity, adj_temp, radial_div, table, mode_values, reciprocal_distance, parts
        )

    arrived = [[] for _ in range(parts)]
    for shift in range(1, row_total):
        sums = partial_sums((row_place + shift) % row_total)
        pairs = [(a, (a + shift) % row_total) for a in range(row_total)]
        for c in range(parts):
            arrived[c].append(lax.ppermute(sums[c], "row", pairs))
    own = partial_sums(row_place)

    returning = jnp.einsum("zj,zk->jk", axial_diff, axial_basis, preferred_element_type=F32)
    forward = jnp.stack(
        [
            axial_basis.reshape(col_total, own_axial, axial_points),
            returning.astype(BF).reshape(col_total, own_axial, axial_points),
        ],
        axis=1,
    )
    axial_blocks = axial_basis.reshape(col_total, own_axial, axial_points)
    radial_values = lax.dynamic_slice_in_dim(radial_eig, col_place * own_count, own_count, 1)

    fits = own_axial % 64 == 0 and own_count % 16 == 0
    outs = []
    new_temp = ()
    for c in range(parts):
        part = slice(c * step, (c + 1) * step)
        hat = radial_forward(own[c], arrived[c], radial_basis, c * step, step, col_total)
        lines = lax.all_to_all(hat, "col", split_axis=0, concat_axis=0, tiled=True)
        if fits:
            returned = axial_solve(
                lines,
                forward.reshape(2 * axial_points, axial_points),
                axial_basis,
                radial_values[part],
                axial_eig,
            )
        else:
            lines = lines.reshape(col_total, step, own_count, 2, 2, own_axial)
            coefficients = jnp.einsum(
                "smxpfy,sfyk->pmxk", lines, forward, preferred_element_type=F32
            )
            coefficients = coefficients / (
                radial_values[part][None, :, :, None] + axial_eig + HEAT_OFFSET
            )
            returned = jnp.einsum(
                "pmxk,syk->smxpy", coefficients.astype(BF), axial_blocks, preferred_element_type=F32
            ).astype(BF)
            returned = returned.reshape(col_total, step, own_count, 2 * own_axial)
        returned = lax.all_to_all(returned, "col", split_axis=0, concat_axis=0, tiled=True)
        if fits:
            new_temp = (radial_back(returned, radial_basis, new_temp, c * step),)
            continue
        returned = jnp.moveaxis(returned, 0, 1).reshape(step, radial_points, 2 * own_axial)
        outs.append(
            jnp.einsum("miw,mri->mwr", returned, radial_basis[part], preferred_element_type=F32).reshape(
                step, 2, own_axial, radial_points
            )
        )
    return new_temp[0] if fits else jnp.concatenate(outs, axis=0)


def solution(mesh):
    in_specs = (
        P(None, "row", "col", None),
        P("row", "col", None),
        P(),
        P(),
        P("row", None, None),
        P("row", None),
        P(),
        P(),
        P(),
    )
    out_specs = P("row", None, "col", None)
    return jax.shard_map(body, mesh=mesh, in_specs=in_specs, out_specs=out_specs, check_vma=False)
```

profile of v0, /device:TPU:11, one launch (start us, length us, event | category | flops | bytes accessed | tf_op | source)
XLA Modules:
  0.0 551.5 jit_solution(10868730012889252469)
XLA Ops:
  3.0 36.8 %sums.3 = (bf16[21,2,2,64,256]{4,3,2,1,0:T(8,128)(2,1)}, bf16[21,2,2,64,256]{4,3,2,1,0:T(8,128)(2,1)}, bf16[21,2,2,64,256]{4,3,2,1,0:T(8,128)(2,1)}, bf16[21,2,2,64,256]{4,3,2,1,0:T(8,128)(2,1)}) custom-call(bf16[3,256,64,256]{3,2,1,0:T(8,128)(2,1)} %vel_ref.3, bf16[256,64,256]{2,1,0:T(8,128)(2,1)} %adj_ref.3, bf16[256,256]{1,0:T(8,128)(2,1)} %div_ref.3, ...), custom_call_target="tpu_custom_call" | custom-call | flops 6576668672 | bytes 33554432 | tf_op jit(solution)/shard_map/sums/pallas_call | solution.py:83
  42.3 36.8 %sums.2 = (bf16[21,2,2,64,256]{4,3,2,1,0:T(8,128)(2,1)}, bf16[21,2,2,64,256]{4,3,2,1,0:T(8,128)(2,1)}, bf16[21,2,2,64,256]{4,3,2,1,0:T(8,128)(2,1)}, bf16[21,2,2,64,256]{4,3,2,1,0:T(8,128)(2,1)}) custom-call(bf16[3,256,64,256]{3,2,1,0:T(8,128)(2,1)} %vel_ref.3, bf16[256,64,256]{2,1,0:T(8,128)(2,1)} %adj_ref.3, bf16[256,256]{1,0:T(8,128)(2,1)} %div_ref.3, ...), custom_call_target="tpu_custom_call" | custom-call | flops 6576668672 | bytes 33554432 | tf_op jit(solution)/shard_map/sums/pallas_call | solution.py:83
  79.1 21.5 %collective-permute-done.refs_1_ = bf16[21,2,2,64,256]{4,3,2,1,0:T(8,128)(2,1)} collective-permute-done((bf16[21,2,2,64,256]{4,3,2,1,0:T(8,128)(2,1)}, bf16[21,2,2,64,256]{4,3,2,1,0:T(8,128)(2,1)}, u32[]{:S(2)}, u32[]{:S(2)}) %collective-permute-start) | collective-permute-done | bytes 2752544 | tf_op jit(solution)/shard_map/ppermute | solution.py:283
  100.6 6.1 %radial.4 = bf16[16,21,16,256]{3,2,1,0:T(8,128)(2,1)} custom-call(bf16[21,2,2,64,256]{4,3,2,1,0:T(8,128)(2,1)} %get-tuple-element.13.refs_0_, bf16[21,2,2,64,256]{4,3,2,1,0:T(8,128)(2,1)} %collective-permute-done.refs_1_, bf16[84,256,256]{2,1,0:T(8,128)(2,1)} %basis_ref.15), custom_call_target="tpu_custom_call" | custom-call | flops 704643072 | bytes 11010048 | tf_op jit(solution)/shard_map/radial/pallas_call | solution.py:133
  106.7 7.4 %all-to-all-start = ((bf16[16,21,16,256]{3,2,1,0:T(8,128)(2,1)}), bf16[16,21,16,256]{3,2,1,0:T(8,128)(2,1)}, u32[]{:S(2)}, u32[]{:S(2)}) async-start(bf16[16,21,16,256]{3,2,1,0:T(8,128)(2,1)} %radial.4), calls=%async_computation | async-start | bytes 5505024 | tf_op jit(solution)/shard_map/all_to_all | solution.py:303
  115.3 59.9 %collective-permute-done.1.refs_1_ = bf16[21,2,2,64,256]{4,3,2,1,0:T(8,128)(2,1)} collective-permute-done((bf16[21,2,2,64,256]{4,3,2,1,0:T(8,128)(2,1)}, bf16[21,2,2,64,256]{4,3,2,1,0:T(8,128)(2,1)}, u32[]{:S(2)}, u32[]{:S(2)}) %collective-permute-start.1) | collective-permute-done | bytes 2752544 | tf_op jit(solution)/shard_map/ppermute | solution.py:283
  175.3 6.1 %radial.5 = bf16[16,21,16,256]{3,2,1,0:T(8,128)(2,1)} custom-call(bf16[21,2,2,64,256]{4,3,2,1,0:T(8,128)(2,1)} %get-tuple-element.15.refs_0_, bf16[21,2,2,64,256]{4,3,2,1,0:T(8,128)(2,1)} %collective-permute-done.1.refs_1_, bf16[84,256,256]{2,1,0:T(8,128)(2,1)} %basis_ref.15), custom_call_target="tpu_custom_call" | custom-call | flops 704643072 | bytes 11010048 | tf_op jit(solution)/shard_map/radial/pallas_call | solution.py:133
  181.3 6.9 %all-to-all-start.2 = ((bf16[16,21,16,256]{3,2,1,0:T(8,128)(2,1)}), bf16[16,21,16,256]{3,2,1,0:T(8,128)(2,1)}, u32[]{:S(2)}, u32[]{:S(2)}) async-start(bf16[16,21,16,256]{3,2,1,0:T(8,128)(2,1)} %radial.5), calls=%async_computation.2 | async-start | bytes 5505024 | tf_op jit(solution)/shard_map/all_to_all | solution.py:303
  189.5 59.9 %collective-permute-done.2.refs_1_ = bf16[21,2,2,64,256]{4,3,2,1,0:T(8,128)(2,1)} collective-permute-done((bf16[21,2,2,64,256]{4,3,2,1,0:T(8,128)(2,1)}, bf16[21,2,2,64,256]{4,3,2,1,0:T(8,128)(2,1)}, u32[]{:S(2)}, u32[]{:S(2)}) %collective-permute-start.2) | collective-permute-done | bytes 2752544 | tf_op jit(solution)/shard_map/ppermute | solution.py:283
  249.4 6.1 %radial.6 = bf16[16,21,16,256]{3,2,1,0:T(8,128)(2,1)} custom-call(bf16[21,2,2,64,256]{4,3,2,1,0:T(8,128)(2,1)} %get-tuple-element.17.refs_0_, bf16[21,2,2,64,256]{4,3,2,1,0:T(8,128)(2,1)} %collective-permute-done.2.refs_1_, bf16[84,256,256]{2,1,0:T(8,128)(2,1)} %basis_ref.15), custom_call_target="tpu_custom_call" | custom-call | flops 704643072 | bytes 11010048 | tf_op jit(solution)/shard_map/radial/pallas_call | solution.py:133
  255.5 6.9 %all-to-all-start.4 = ((bf16[16,21,16,256]{3,2,1,0:T(8,128)(2,1)}), bf16[16,21,16,256]{3,2,1,0:T(8,128)(2,1)}, u32[]{:S(2)}, u32[]{:S(2)}) async-start(bf16[16,21,16,256]{3,2,1,0:T(8,128)(2,1)} %radial.6), calls=%async_computation.4 | async-start | bytes 5505024 | tf_op jit(solution)/shard_map/all_to_all | solution.py:303
  263.6 59.9 %collective-permute-done.3.refs_1_ = bf16[21,2,2,64,256]{4,3,2,1,0:T(8,128)(2,1)} collective-permute-done((bf16[21,2,2,64,256]{4,3,2,1,0:T(8,128)(2,1)}, bf16[21,2,2,64,256]{4,3,2,1,0:T(8,128)(2,1)}, u32[]{:S(2)}, u32[]{:S(2)}) %collective-permute-start.3) | collective-permute-done | bytes 2752544 | tf_op jit(solution)/shard_map/ppermute | solution.py:283
  323.6 6.1 %radial.7 = bf16[16,21,16,256]{3,2,1,0:T(8,128)(2,1)} custom-call(bf16[21,2,2,64,256]{4,3,2,1,0:T(8,128)(2,1)} %get-tuple-element.19.refs_0_, bf16[21,2,2,64,256]{4,3,2,1,0:T(8,128)(2,1)} %collective-permute-done.3.refs_1_, bf16[84,256,256]{2,1,0:T(8,128)(2,1)} %basis_ref.15), custom_call_target="tpu_custom_call" | custom-call | flops 704643072 | bytes 11010048 | tf_op jit(solution)/shard_map/radial/pallas_call | solution.py:133
  329.7 7.0 %all-to-all-start.6 = ((bf16[16,21,16,256]{3,2,1,0:T(8,128)(2,1)}), bf16[16,21,16,256]{3,2,1,0:T(8,128)(2,1)}, u32[]{:S(2)}, u32[]{:S(2)}) async-start(bf16[16,21,16,256]{3,2,1,0:T(8,128)(2,1)} %radial.7), calls=%async_computation.6 | async-start | bytes 5505024 | tf_op jit(solution)/shard_map/all_to_all | solution.py:303
  337.6 4.1 convolution_convert_fusion
  344.1 9.5 %axial.5 = bf16[16,21,16,128]{3,2,1,0:T(8,128)(2,1)} custom-call(bf16[16,21,16,256]{3,2,1,0:T(8,128)(2,1)} %all-to-all-done.2.lines_ref, bf16[2048,1024]{1,0:T(8,128)(2,1)} %bitcast.16, bf16[1024,1024]{1,0:T(8,128)(2,1)} %basis_ref.11, f32[336,1]{1,0:T(8,128)} %reshape.316.radial_ref, f32[1,1024]{1,0:T(1,128)} %bitcast.24), custom_call_target="tpu_custom_call" | custom-call | flops 4227858432 | bytes 8355840 | tf_op jit(solution)/shard_map/axial/pallas_call | solution.py:190
  353.6 44.6 %all-to-all-done.6.lines_ref = bf16[16,21,16,256]{3,2,1,0:T(8,128)(2,1)} async-done(((bf16[16,21,16,256]{3,2,1,0:T(8,128)(2,1)}), bf16[16,21,16,256]{3,2,1,0:T(8,128)(2,1)}, u32[]{:S(2)}, u32[]{:S(2)}) %all-to-all-start.6) | async-done | bytes 2752544 | tf_op jit(solution)/shard_map/all_to_all | solution.py:303
  398.3 4.8 all-to-all-start.3
  403.8 9.6 %axial.6 = bf16[16,21,16,128]{3,2,1,0:T(8,128)(2,1)} custom-call(bf16[16,21,16,256]{3,2,1,0:T(8,128)(2,1)} %all-to-all-done.4.lines_ref, bf16[2048,1024]{1,0:T(8,128)(2,1)} %bitcast.17, bf16[1024,1024]{1,0:T(8,128)(2,1)} %basis_ref.11, f32[336,1]{1,0:T(8,128)} %reshape.317.radial_ref, f32[1,1024]{1,0:T(1,128)} %bitcast.25), custom_call_target="tpu_custom_call" | custom-call | flops 4227858432 | bytes 8355840 | tf_op jit(solution)/shard_map/axial/pallas_call | solution.py:190
  413.4 21.6 %all-to-all-done.3.returned_ref = bf16[16,21,16,128]{3,2,1,0:T(8,128)(2,1)S(1)} async-done(((bf16[16,21,16,128]{3,2,1,0:T(8,128)(2,1)}), bf16[16,21,16,128]{3,2,1,0:T(8,128)(2,1)S(1)}, u32[]{:S(2)}, u32[]{:S(2)}) %all-to-all-start.3) | async-done | bytes 1376288 | tf_op jit(solution)/shard_map/all_to_all | solution.py:324
  435.0 4.7 all-to-all-start.5
  440.5 9.6 %axial.7 = bf16[16,21,16,128]{3,2,1,0:T(8,128)(2,1)} custom-call(bf16[16,21,16,256]{3,2,1,0:T(8,128)(2,1)} %all-to-all-done.6.lines_ref, bf16[2048,1024]{1,0:T(8,128)(2,1)} %bitcast.18, bf16[1024,1024]{1,0:T(8,128)(2,1)} %basis_ref.11, f32[336,1]{1,0:T(8,128)} %reshape.318.radial_ref, f32[1,1024]{1,0:T(1,128)} %bitcast.26), custom_call_target="tpu_custom_call" | custom-call | flops 4227858432 | bytes 8355840 | tf_op jit(solution)/shard_map/axial/pallas_call | solution.py:190
  450.1 21.6 %all-to-all-done.5.returned_ref = bf16[16,21,16,128]{3,2,1,0:T(8,128)(2,1)S(1)} async-done(((bf16[16,21,16,128]{3,2,1,0:T(8,128)(2,1)}), bf16[16,21,16,128]{3,2,1,0:T(8,128)(2,1)S(1)}, u32[]{:S(2)}, u32[]{:S(2)}) %all-to-all-start.5) | async-done | bytes 1376288 | tf_op jit(solution)/shard_map/all_to_all | solution.py:324
  471.7 4.7 all-to-all-start.7
  477.3 9.5 %axial.4 = bf16[16,21,16,128]{3,2,1,0:T(8,128)(2,1)} custom-call(bf16[16,21,16,256]{3,2,1,0:T(8,128)(2,1)} %all-to-all-done.lines_ref, bf16[2048,1024]{1,0:T(8,128)(2,1)} %bitcast.19, bf16[1024,1024]{1,0:T(8,128)(2,1)} %basis_ref.11, f32[336,1]{1,0:T(8,128)} %reshape.315.radial_ref, f32[1,1024]{1,0:T(1,128)} %bitcast.27), custom_call_target="tpu_custom_call" | custom-call | flops 4227858432 | bytes 8355840 | tf_op jit(solution)/shard_map/axial/pallas_call | solution.py:190
  486.8 21.6 %all-to-all-done.7.returned_ref = bf16[16,21,16,128]{3,2,1,0:T(8,128)(2,1)S(1)} async-done(((bf16[16,21,16,128]{3,2,1,0:T(8,128)(2,1)}), bf16[16,21,16,128]{3,2,1,0:T(8,128)(2,1)S(1)}, u32[]{:S(2)}, u32[]{:S(2)}) %all-to-all-start.7) | async-done | bytes 1376288 | tf_op jit(solution)/shard_map/all_to_all | solution.py:324
  508.4 4.7 all-to-all-start.1
  513.2 5.2 last.4.refs_0_
  518.3 5.2 last.5.refs_0_
  523.5 5.2 last.6.refs_0_
  528.7 16.4 %all-to-all-done.1.returned_ref = bf16[16,21,16,128]{3,2,1,0:T(8,128)(2,1)S(1)} async-done(((bf16[16,21,16,128]{3,2,1,0:T(8,128)(2,1)}), bf16[16,21,16,128]{3,2,1,0:T(8,128)(2,1)S(1)}, u32[]{:S(2)}, u32[]{:S(2)}) %all-to-all-start.1) | async-done | bytes 1376288 | tf_op jit(solution)/shard_map/all_to_all | solution.py:324
  546.2 5.3 last.7
  (40 shorter events, 16.0 us)
Async XLA Ops:
  0.0 337.6 %copy-start = (bf16[1024,1024]{1,0:T(8,128)(2,1)S(1)}, bf16[1024,1024]{1,0:T(8,128)(2,1)}, u32[]{:S(2)}) copy-start(bf16[1024,1024]{1,0:T(8,128)(2,1)} %param.15) | copy-start | bytes 6291460
  39.8 60.9 %collective-permute-start = (bf16[21,2,2,64,256]{4,3,2,1,0:T(8,128)(2,1)}, bf16[21,2,2,64,256]{4,3,2,1,0:T(8,128)(2,1)}, u32[]{:S(2)}, u32[]{:S(2)}) collective-permute-start(bf16[21,2,2,64,256]{4,3,2,1,0:T(8,128)(2,1)} %get-tuple-element.14), channel_id=1, source_target_pairs={{0,16},{16,0},{1,17},{17,1},{2,18},{18,2},{3,19},{19,3},{4,20},{20... | collective-permute-start | bytes 8257544 | tf_op jit(solution)/shard_map/ppermute | solution.py:283
  106.7 74.6 %all-to-all-start = ((bf16[16,21,16,256]{3,2,1,0:T(8,128)(2,1)}), bf16[16,21,16,256]{3,2,1,0:T(8,128)(2,1)}, u32[]{:S(2)}, u32[]{:S(2)}) async-start(bf16[16,21,16,256]{3,2,1,0:T(8,128)(2,1)} %radial.4), calls=%async_computation | async-start | bytes 5505024 | tf_op jit(solution)/shard_map/all_to_all | solution.py:303
  114.1 61.2 %collective-permute-start.1 = (bf16[21,2,2,64,256]{4,3,2,1,0:T(8,128)(2,1)}, bf16[21,2,2,64,256]{4,3,2,1,0:T(8,128)(2,1)}, u32[]{:S(2)}, u32[]{:S(2)}) collective-permute-start(bf16[21,2,2,64,256]{4,3,2,1,0:T(8,128)(2,1)} %get-tuple-element.16), channel_id=1, source_target_pairs={{0,16},{16,0},{1,17},{17,1},{2,18},{18,2},{3,19},{19,3},{4,20},{20... | collective-permute-start | bytes 8257544 | tf_op jit(solution)/shard_map/ppermute | solution.py:283
  181.3 74.2 %all-to-all-start.2 = ((bf16[16,21,16,256]{3,2,1,0:T(8,128)(2,1)}), bf16[16,21,16,256]{3,2,1,0:T(8,128)(2,1)}, u32[]{:S(2)}, u32[]{:S(2)}) async-start(bf16[16,21,16,256]{3,2,1,0:T(8,128)(2,1)} %radial.5), calls=%async_computation.2 | async-start | bytes 5505024 | tf_op jit(solution)/shard_map/all_to_all | solution.py:303
  188.2 61.2 %collective-permute-start.2 = (bf16[21,2,2,64,256]{4,3,2,1,0:T(8,128)(2,1)}, bf16[21,2,2,64,256]{4,3,2,1,0:T(8,128)(2,1)}, u32[]{:S(2)}, u32[]{:S(2)}) collective-permute-start(bf16[21,2,2,64,256]{4,3,2,1,0:T(8,128)(2,1)} %get-tuple-element.18), channel_id=1, source_target_pairs={{0,16},{16,0},{1,17},{17,1},{2,18},{18,2},{3,19},{19,3},{4,20},{20... | collective-permute-start | bytes 8257544 | tf_op jit(solution)/shard_map/ppermute | solution.py:283
  255.5 74.1 %all-to-all-start.4 = ((bf16[16,21,16,256]{3,2,1,0:T(8,128)(2,1)}), bf16[16,21,16,256]{3,2,1,0:T(8,128)(2,1)}, u32[]{:S(2)}, u32[]{:S(2)}) async-start(bf16[16,21,16,256]{3,2,1,0:T(8,128)(2,1)} %radial.6), calls=%async_computation.4 | async-start | bytes 5505024 | tf_op jit(solution)/shard_map/all_to_all | solution.py:303
  262.4 61.2 %collective-permute-start.3 = (bf16[21,2,2,64,256]{4,3,2,1,0:T(8,128)(2,1)}, bf16[21,2,2,64,256]{4,3,2,1,0:T(8,128)(2,1)}, u32[]{:S(2)}, u32[]{:S(2)}) collective-permute-start(bf16[21,2,2,64,256]{4,3,2,1,0:T(8,128)(2,1)} %get-tuple-element.20), channel_id=1, source_target_pairs={{0,16},{16,0},{1,17},{17,1},{2,18},{18,2},{3,19},{19,3},{4,20},{20... | collective-permute-start | bytes 8257544 | tf_op jit(solution)/shard_map/ppermute | solution.py:283
  329.7 7.0 %copy-start.7 = (f32[84,256]{1,0:T(8,128)S(1)}, f32[84,256]{1,0:T(8,128)}, u32[]{:S(2)}) copy-start(f32[84,256]{1,0:T(8,128)} %param.14) | copy-start | bytes 258052
  329.7 68.6 %all-to-all-start.6 = ((bf16[16,21,16,256]{3,2,1,0:T(8,128)(2,1)}), bf16[16,21,16,256]{3,2,1,0:T(8,128)(2,1)}, u32[]{:S(2)}, u32[]{:S(2)}) async-start(bf16[16,21,16,256]{3,2,1,0:T(8,128)(2,1)} %radial.7), calls=%async_computation.6 | async-start | bytes 5505024 | tf_op jit(solution)/shard_map/all_to_all | solution.py:303
  337.6 4.1 copy-start.6
  398.3 36.7 %all-to-all-start.3 = ((bf16[16,21,16,128]{3,2,1,0:T(8,128)(2,1)}), bf16[16,21,16,128]{3,2,1,0:T(8,128)(2,1)S(1)}, u32[]{:S(2)}, u32[]{:S(2)}) async-start(bf16[16,21,16,128]{3,2,1,0:T(8,128)(2,1)} %axial.5), calls=%async_computation.3 | async-start | bytes 2752512 | tf_op jit(solution)/shard_map/all_to_all | solution.py:324
  435.0 15.1 %copy-start.2 = (bf16[16,21,16,128]{3,2,1,0:T(8,128)(2,1)}, bf16[16,21,16,128]{3,2,1,0:T(8,128)(2,1)S(1)}, u32[]{:S(2)}) copy-start(bf16[16,21,16,128]{3,2,1,0:T(8,128)(2,1)S(1)} %all-to-all-done.3.returned_ref) | copy-start | bytes 4128772
  435.0 36.7 %all-to-all-start.5 = ((bf16[16,21,16,128]{3,2,1,0:T(8,128)(2,1)}), bf16[16,21,16,128]{3,2,1,0:T(8,128)(2,1)S(1)}, u32[]{:S(2)}, u32[]{:S(2)}) async-start(bf16[16,21,16,128]{3,2,1,0:T(8,128)(2,1)} %axial.6), calls=%async_computation.5 | async-start | bytes 2752512 | tf_op jit(solution)/shard_map/all_to_all | solution.py:324
  471.7 15.1 %copy-start.3 = (bf16[16,21,16,128]{3,2,1,0:T(8,128)(2,1)}, bf16[16,21,16,128]{3,2,1,0:T(8,128)(2,1)S(1)}, u32[]{:S(2)}) copy-start(bf16[16,21,16,128]{3,2,1,0:T(8,128)(2,1)S(1)} %all-to-all-done.5.returned_ref) | copy-start | bytes 4128772
  471.7 36.7 %all-to-all-start.7 = ((bf16[16,21,16,128]{3,2,1,0:T(8,128)(2,1)}), bf16[16,21,16,128]{3,2,1,0:T(8,128)(2,1)S(1)}, u32[]{:S(2)}, u32[]{:S(2)}) async-start(bf16[16,21,16,128]{3,2,1,0:T(8,128)(2,1)} %axial.7), calls=%async_computation.7 | async-start | bytes 2752512 | tf_op jit(solution)/shard_map/all_to_all | solution.py:324
  508.4 4.7 copy-start.5
  508.4 36.7 %all-to-all-start.1 = ((bf16[16,21,16,128]{3,2,1,0:T(8,128)(2,1)}), bf16[16,21,16,128]{3,2,1,0:T(8,128)(2,1)S(1)}, u32[]{:S(2)}, u32[]{:S(2)}) async-start(bf16[16,21,16,128]{3,2,1,0:T(8,128)(2,1)} %axial.4), calls=%async_computation.1 | async-start | bytes 2752512 | tf_op jit(solution)/shard_map/all_to_all | solution.py:324
  545.1 1.1 copy-start.4
  546.2 5.3 copy-start.1
where the time goes:
time: 553 us; the launch traced here: 552 us
  waiting for transfers between devices  327 us (59%)
  Pallas kernels  157 us (28%)
  starting transfers between devices  52.1 us (9%)
  local copies, waits for them, and re-layouts  7.01 us (1%)
    ppermute x4, waiting for transfers between devices, body(): arrived[c].append(lax.ppermute(sums[c], 'row', pairs))  201 us
    all_to_all x4, waiting for transfers between devices, body(): lax.all_to_all(returned, 'col', split_axis=0, concat_axis=0, tiled=True)  81.3 us
    pallas_call x2, Pallas kernels, azimuth_sums(): pl.pallas_call(functools.partial(sums_kernel, modes, padded), grid=(own_a...  73.6 us
    all_to_all x4, waiting for transfers between devices, body(): lines = lax.all_to_all(hat, 'col', split_axis=0, concat_axis=0, tiled=True)  44.6 us
    pallas_call x4, Pallas kernels, axial_solve(): pl.pallas_call(axial_kernel, grid=(step // count,), in_specs=[pl.BlockSpe...  38.2 us
    all_to_all x4, starting transfers between devices, body(): lines = lax.all_to_all(hat, 'col', split_axis=0, concat_axis=0, tiled=True)  28.1 us
    pallas_call x4, Pallas kernels, radial_forward(): pl.pallas_call(functools.partial(radial_kernel, count), grid=(step // cou...  24.4 us
    pallas_call x4, Pallas kernels, radial_back(): pl.pallas_call(functools.partial(last_kernel, count), grid=(step // count...  20.8 us
  transfers between devices with their start and end apart: 12, of which 9 were waited for; matrix products, arithmetic and copies ran while one was open for 2% of the time, Pallas kernels for 20%

commit v1 on v0

--- a/solution.py
+++ b/solution.py
@@ -271,9 +271,17 @@
     def partial_sums(place):
         table = wave_rows(place * modes, modes, row_place * angles, angles, circle)
         mode_values = (place * modes + jnp.arange(modes, dtype=jnp.int32)).astype(F32)
-        return azimuth_sums(
-            velocity, adj_temp, radial_div, table, mode_values, reciprocal_distance, parts
-        )
+
+        def some(where, count):
+            return azimuth_sums(
+                velocity, adj_temp, radial_div, table[where], mode_values[where],
+                reciprocal_distance, count,
+            )
+
+        sums = list(some(slice(0, step), 1))
+        if parts > 1:
+            sums += some(slice(step, modes), parts - 1)
+        return sums
 
     arrived = [[] for _ in range(parts)]
     for shift in range(1, row_total):

time: 553 us -> 582 us (1.052)
  Pallas kernels: 157 us -> 212 us
  waiting for transfers between devices: 327 us -> 298 us
    pallas_call x2 -> x4, Pallas kernels: 73.6 us -> 129 us  [azimuth_sums(): pl.pallas_call(functools.partial(sums_kernel, modes, padded), grid=(own_a...]
    ppermute x4, waiting for transfers between devices: 201 us -> 172 us  [body(): arrived[c].append(lax.ppermute(sums[c], 'row', pairs))]
  transfers between devices with their start and end apart: 12 -> 12, of which waited for: 9 -> 9; matrix products, arithmetic and copies ran while one was open for 2% -> 2% of each run, Pallas kernels for 20% -> 29%
where the time goes in v1:
time: 582 us; the launch traced here: 581 us
  waiting for transfers between devices  298 us (51%)
  Pallas kernels  212 us (36%)
  starting transfers between devices  52.2 us (9%)
  local copies, waits for them, and re-layouts  9.5 us (2%)
    ppermute x4, waiting for transfers between devices, body(): arrived[c].append(lax.ppermute(sums[c], 'row', pairs))  172 us
    pallas_call x4, Pallas kernels, azimuth_sums(): pl.pallas_call(functools.partial(sums_kernel, modes, padded), grid=(own_a...  129 us
    all_to_all x4, waiting for transfers between devices, body(): lax.all_to_all(returned, 'col', split_axis=0, concat_axis=0, tiled=True)  81.4 us
    all_to_all x4, waiting for transfers between devices, body(): lines = lax.all_to_all(hat, 'col', split_axis=0, concat_axis=0, tiled=True)  44.6 us
    pallas_call x4, Pallas kernels, axial_solve(): pl.pallas_call(axial_kernel, grid=(step // count,), in_specs=[pl.BlockSpe...  38.2 us
    all_to_all x4, starting transfers between devices, body(): lines = lax.all_to_all(hat, 'col', split_axis=0, concat_axis=0, tiled=True)  28.3 us
    pallas_call x4, Pallas kernels, radial_forward(): pl.pallas_call(functools.partial(radial_kernel, count), grid=(step // cou...  24.3 us
    pallas_call x4, Pallas kernels, radial_back(): pl.pallas_call(functools.partial(last_kernel, count), grid=(step // count...  20.8 us
  transfers between devices with their start and end apart: 12, of which 9 were waited for; matrix products, arithmetic and copies ran while one was open for 2% of the time, Pallas kernels for 29%

profile of v1, /device:TPU:11, one launch (start us, length us, event | category | flops | bytes accessed | tf_op | source)
XLA Modules:
  0.0 581.0 jit_solution(4275744063505383963)
XLA Ops:
  3.0 30.5 %sums.7 = bf16[21,2,2,64,256]{4,3,2,1,0:T(8,128)(2,1)} custom-call(bf16[3,256,64,256]{3,2,1,0:T(8,128)(2,1)} %vel_ref.7, bf16[256,64,256]{2,1,0:T(8,128)(2,1)} %adj_ref.7, bf16[256,256]{1,0:T(8,128)(2,1)} %div_ref.7, bf16[48,256]{1,0:T(8,128)(2,1)} %bitcast.32, f32[24,256]{1,0:T(8,128)} %pad.35.scale_ref), custom_call_target="tpu_custom_call" | custom-call | flops 3355443200 | bytes 33554432 | tf_op jit(solution)/shard_map/sums/pallas_call | solution.py:83
  36.0 30.4 %sums.6.refs_0_ = bf16[21,2,2,64,256]{4,3,2,1,0:T(8,128)(2,1)} custom-call(bf16[3,256,64,256]{3,2,1,0:T(8,128)(2,1)} %vel_ref.7, bf16[256,64,256]{2,1,0:T(8,128)(2,1)} %adj_ref.7, bf16[256,256]{1,0:T(8,128)(2,1)} %div_ref.7, bf16[48,256]{1,0:T(8,128)(2,1)} %bitcast.33, f32[24,256]{1,0:T(8,128)} %pad.33.scale_ref), custom_call_target="tpu_custom_call" | custom-call | flops 3355443200 | bytes 33554432 | tf_op jit(solution)/shard_map/sums/pallas_call | solution.py:83
  66.4 28.0 %collective-permute-done.3.refs_1_ = bf16[21,2,2,64,256]{4,3,2,1,0:T(8,128)(2,1)} collective-permute-done((bf16[21,2,2,64,256]{4,3,2,1,0:T(8,128)(2,1)}, bf16[21,2,2,64,256]{4,3,2,1,0:T(8,128)(2,1)}, u32[]{:S(2)}, u32[]{:S(2)}) %collective-permute-start.3) | collective-permute-done | bytes 2752544 | tf_op jit(solution)/shard_map/ppermute | solution.py:291
  94.4 6.1 %radial.7 = bf16[16,21,16,256]{3,2,1,0:T(8,128)(2,1)} custom-call(bf16[21,2,2,64,256]{4,3,2,1,0:T(8,128)(2,1)} %sums.6.refs_0_, bf16[21,2,2,64,256]{4,3,2,1,0:T(8,128)(2,1)} %collective-permute-done.3.refs_1_, bf16[84,256,256]{2,1,0:T(8,128)(2,1)} %basis_ref.15), custom_call_target="tpu_custom_call" | custom-call | flops 704643072 | bytes 11010048 | tf_op jit(solution)/shard_map/radial/pallas_call | solution.py:133
  100.4 7.5 %all-to-all-start.6 = ((bf16[16,21,16,256]{3,2,1,0:T(8,128)(2,1)}), bf16[16,21,16,256]{3,2,1,0:T(8,128)(2,1)}, u32[]{:S(2)}, u32[]{:S(2)}) async-start(bf16[16,21,16,256]{3,2,1,0:T(8,128)(2,1)} %radial.7), calls=%async_computation.6 | async-start | bytes 5505024 | tf_op jit(solution)/shard_map/all_to_all | solution.py:311
  109.5 34.1 %sums.5 = (bf16[21,2,2,64,256]{4,3,2,1,0:T(8,128)(2,1)}, bf16[21,2,2,64,256]{4,3,2,1,0:T(8,128)(2,1)}, bf16[21,2,2,64,256]{4,3,2,1,0:T(8,128)(2,1)}) custom-call(bf16[3,256,64,256]{3,2,1,0:T(8,128)(2,1)} %vel_ref.7, bf16[256,64,256]{2,1,0:T(8,128)(2,1)} %adj_ref.7, bf16[256,256]{1,0:T(8,128)(2,1)} %div_ref.7, bf16[128,256]{1,0:T(8,128)(2,1)} %bitcast.31, ...), custom_call_target="tpu_custom_call" | custom-call | flops 5368709120 | bytes 33554432 | tf_op jit(solution)/shard_map/sums/pallas_call | solution.py:83
  146.1 34.1 %sums.4 = (bf16[21,2,2,64,256]{4,3,2,1,0:T(8,128)(2,1)}, bf16[21,2,2,64,256]{4,3,2,1,0:T(8,128)(2,1)}, bf16[21,2,2,64,256]{4,3,2,1,0:T(8,128)(2,1)}) custom-call(bf16[3,256,64,256]{3,2,1,0:T(8,128)(2,1)} %vel_ref.7, bf16[256,64,256]{2,1,0:T(8,128)(2,1)} %adj_ref.7, bf16[256,256]{1,0:T(8,128)(2,1)} %div_ref.7, bf16[128,256]{1,0:T(8,128)(2,1)} %bitcast.30, ...), custom_call_target="tpu_custom_call" | custom-call | flops 5368709120 | bytes 33554432 | tf_op jit(solution)/shard_map/sums/pallas_call | solution.py:83
  180.2 24.5 %collective-permute-done.refs_1_ = bf16[21,2,2,64,256]{4,3,2,1,0:T(8,128)(2,1)} collective-permute-done((bf16[21,2,2,64,256]{4,3,2,1,0:T(8,128)(2,1)}, bf16[21,2,2,64,256]{4,3,2,1,0:T(8,128)(2,1)}, u32[]{:S(2)}, u32[]{:S(2)}) %collective-permute-start) | collective-permute-done | bytes 2752544 | tf_op jit(solution)/shard_map/ppermute | solution.py:291
  204.7 6.1 %radial.4 = bf16[16,21,16,256]{3,2,1,0:T(8,128)(2,1)} custom-call(bf16[21,2,2,64,256]{4,3,2,1,0:T(8,128)(2,1)} %get-tuple-element.11.refs_0_, bf16[21,2,2,64,256]{4,3,2,1,0:T(8,128)(2,1)} %collective-permute-done.refs_1_, bf16[84,256,256]{2,1,0:T(8,128)(2,1)} %basis_ref.15), custom_call_target="tpu_custom_call" | custom-call | flops 704643072 | bytes 11010048 | tf_op jit(solution)/shard_map/radial/pallas_call | solution.py:133
  210.8 6.9 %all-to-all-start = ((bf16[16,21,16,256]{3,2,1,0:T(8,128)(2,1)}), bf16[16,21,16,256]{3,2,1,0:T(8,128)(2,1)}, u32[]{:S(2)}, u32[]{:S(2)}) async-start(bf16[16,21,16,256]{3,2,1,0:T(8,128)(2,1)} %radial.4), calls=%async_computation | async-start | bytes 5505024 | tf_op jit(solution)/shard_map/all_to_all | solution.py:311
  218.9 59.9 %collective-permute-done.1.refs_1_ = bf16[21,2,2,64,256]{4,3,2,1,0:T(8,128)(2,1)} collective-permute-done((bf16[21,2,2,64,256]{4,3,2,1,0:T(8,128)(2,1)}, bf16[21,2,2,64,256]{4,3,2,1,0:T(8,128)(2,1)}, u32[]{:S(2)}, u32[]{:S(2)}) %collective-permute-start.1) | collective-permute-done | bytes 2752544 | tf_op jit(solution)/shard_map/ppermute | solution.py:291
  278.8 6.1 %radial.5 = bf16[16,21,16,256]{3,2,1,0:T(8,128)(2,1)} custom-call(bf16[21,2,2,64,256]{4,3,2,1,0:T(8,128)(2,1)} %get-tuple-element.13.refs_0_, bf16[21,2,2,64,256]{4,3,2,1,0:T(8,128)(2,1)} %collective-permute-done.1.refs_1_, bf16[84,256,256]{2,1,0:T(8,128)(2,1)} %basis_ref.15), custom_call_target="tpu_custom_call" | custom-call | flops 704643072 | bytes 11010048 | tf_op jit(solution)/shard_map/radial/pallas_call | solution.py:133
  284.9 6.9 %all-to-all-start.2 = ((bf16[16,21,16,256]{3,2,1,0:T(8,128)(2,1)}), bf16[16,21,16,256]{3,2,1,0:T(8,128)(2,1)}, u32[]{:S(2)}, u32[]{:S(2)}) async-start(bf16[16,21,16,256]{3,2,1,0:T(8,128)(2,1)} %radial.5), calls=%async_computation.2 | async-start | bytes 5505024 | tf_op jit(solution)/shard_map/all_to_all | solution.py:311
  293.0 59.9 %collective-permute-done.2.refs_1_ = bf16[21,2,2,64,256]{4,3,2,1,0:T(8,128)(2,1)} collective-permute-done((bf16[21,2,2,64,256]{4,3,2,1,0:T(8,128)(2,1)}, bf16[21,2,2,64,256]{4,3,2,1,0:T(8,128)(2,1)}, u32[]{:S(2)}, u32[]{:S(2)}) %collective-permute-start.2) | collective-permute-done | bytes 2752544 | tf_op jit(solution)/shard_map/ppermute | solution.py:291
  352.9 6.1 %radial.6 = bf16[16,21,16,256]{3,2,1,0:T(8,128)(2,1)} custom-call(bf16[21,2,2,64,256]{4,3,2,1,0:T(8,128)(2,1)} %get-tuple-element.15.refs_0_, bf16[21,2,2,64,256]{4,3,2,1,0:T(8,128)(2,1)} %collective-permute-done.2.refs_1_, bf16[84,256,256]{2,1,0:T(8,128)(2,1)} %basis_ref.15), custom_call_target="tpu_custom_call" | custom-call | flops 704643072 | bytes 11010048 | tf_op jit(solution)/shard_map/radial/pallas_call | solution.py:133
  359.0 7.0 %all-to-all-start.4 = ((bf16[16,21,16,256]{3,2,1,0:T(8,128)(2,1)}), bf16[16,21,16,256]{3,2,1,0:T(8,128)(2,1)}, u32[]{:S(2)}, u32[]{:S(2)}) async-start(bf16[16,21,16,256]{3,2,1,0:T(8,128)(2,1)} %radial.6), calls=%async_computation.4 | async-start | bytes 5505024 | tf_op jit(solution)/shard_map/all_to_all | solution.py:311
  373.5 9.5 %axial.7 = bf16[16,21,16,128]{3,2,1,0:T(8,128)(2,1)} custom-call(bf16[16,21,16,256]{3,2,1,0:T(8,128)(2,1)} %all-to-all-done.6.lines_ref, bf16[2048,1024]{1,0:T(8,128)(2,1)} %bitcast.24, bf16[1024,1024]{1,0:T(8,128)(2,1)} %basis_ref.11, f32[336,1]{1,0:T(8,128)} %reshape.324.radial_ref, f32[1,1024]{1,0:T(1,128)} %bitcast.36), custom_call_target="tpu_custom_call" | custom-call | flops 4227858432 | bytes 8355840 | tf_op jit(solution)/shard_map/axial/pallas_call | solution.py:190
  383.0 44.6 %all-to-all-done.4.lines_ref = bf16[16,21,16,256]{3,2,1,0:T(8,128)(2,1)} async-done(((bf16[16,21,16,256]{3,2,1,0:T(8,128)(2,1)}), bf16[16,21,16,256]{3,2,1,0:T(8,128)(2,1)}, u32[]{:S(2)}, u32[]{:S(2)}) %all-to-all-start.4) | async-done | bytes 2752544 | tf_op jit(solution)/shard_map/all_to_all | solution.py:311
  427.6 4.8 all-to-all-start.7
  433.2 9.6 %axial.5 = bf16[16,21,16,128]{3,2,1,0:T(8,128)(2,1)} custom-call(bf16[16,21,16,256]{3,2,1,0:T(8,128)(2,1)} %all-to-all-done.2.lines_ref, bf16[2048,1024]{1,0:T(8,128)(2,1)} %bitcast.25, bf16[1024,1024]{1,0:T(8,128)(2,1)} %basis_ref.11, f32[336,1]{1,0:T(8,128)} %reshape.322.radial_ref, f32[1,1024]{1,0:T(1,128)} %bitcast.37), custom_call_target="tpu_custom_call" | custom-call | flops 4227858432 | bytes 8355840 | tf_op jit(solution)/shard_map/axial/pallas_call | solution.py:190
  442.7 21.6 %all-to-all-done.7.returned_ref = bf16[16,21,16,128]{3,2,1,0:T(8,128)(2,1)S(1)} async-done(((bf16[16,21,16,128]{3,2,1,0:T(8,128)(2,1)}), bf16[16,21,16,128]{3,2,1,0:T(8,128)(2,1)S(1)}, u32[]{:S(2)}, u32[]{:S(2)}) %all-to-all-start.7) | async-done | bytes 1376288 | tf_op jit(solution)/shard_map/all_to_all | solution.py:332
  471.0 9.5 %axial.6 = bf16[16,21,16,128]{3,2,1,0:T(8,128)(2,1)} custom-call(bf16[16,21,16,256]{3,2,1,0:T(8,128)(2,1)} %all-to-all-done.4.lines_ref, bf16[2048,1024]{1,0:T(8,128)(2,1)} %bitcast.26, bf16[1024,1024]{1,0:T(8,128)(2,1)} %basis_ref.11, f32[336,1]{1,0:T(8,128)} %reshape.323.radial_ref, f32[1,1024]{1,0:T(1,128)} %bitcast.38), custom_call_target="tpu_custom_call" | custom-call | flops 4227858432 | bytes 8355840 | tf_op jit(solution)/shard_map/axial/pallas_call | solution.py:190
  480.6 21.6 %all-to-all-done.3.returned_ref = bf16[16,21,16,128]{3,2,1,0:T(8,128)(2,1)S(1)} async-done(((bf16[16,21,16,128]{3,2,1,0:T(8,128)(2,1)}), bf16[16,21,16,128]{3,2,1,0:T(8,128)(2,1)S(1)}, u32[]{:S(2)}, u32[]{:S(2)}) %all-to-all-start.3) | async-done | bytes 1376288 | tf_op jit(solution)/shard_map/all_to_all | solution.py:332
  502.2 4.7 all-to-all-start.5
  507.7 9.5 %axial.4 = bf16[16,21,16,128]{3,2,1,0:T(8,128)(2,1)} custom-call(bf16[16,21,16,256]{3,2,1,0:T(8,128)(2,1)} %all-to-all-done.lines_ref, bf16[2048,1024]{1,0:T(8,128)(2,1)} %bitcast.27, bf16[1024,1024]{1,0:T(8,128)(2,1)} %basis_ref.11, f32[336,1]{1,0:T(8,128)} %reshape.321.radial_ref, f32[1,1024]{1,0:T(1,128)} %bitcast.39), custom_call_target="tpu_custom_call" | custom-call | flops 4227858432 | bytes 8355840 | tf_op jit(solution)/shard_map/axial/pallas_call | solution.py:190
  517.3 21.6 %all-to-all-done.5.returned_ref = bf16[16,21,16,128]{3,2,1,0:T(8,128)(2,1)S(1)} async-done(((bf16[16,21,16,128]{3,2,1,0:T(8,128)(2,1)}), bf16[16,21,16,128]{3,2,1,0:T(8,128)(2,1)S(1)}, u32[]{:S(2)}, u32[]{:S(2)}) %all-to-all-start.5) | async-done | bytes 1376288 | tf_op jit(solution)/shard_map/all_to_all | solution.py:332
  538.9 4.7 all-to-all-start.1
  543.6 5.2 last.4.refs_0_
  548.8 5.2 last.5.refs_0_
  554.0 5.2 last.6.refs_0_
  559.2 16.5 %all-to-all-done.1.returned_ref = bf16[16,21,16,128]{3,2,1,0:T(8,128)(2,1)} async-done(((bf16[16,21,16,128]{3,2,1,0:T(8,128)(2,1)}), bf16[16,21,16,128]{3,2,1,0:T(8,128)(2,1)}, u32[]{:S(2)}, u32[]{:S(2)}) %all-to-all-start.1) | async-done | bytes 1376288 | tf_op jit(solution)/shard_map/all_to_all | solution.py:332
  575.7 5.3 last.7
  (51 shorter events, 27.6 us)
Async XLA Ops:
  0.0 366.9 %copy-start = (bf16[1024,1024]{1,0:T(8,128)(2,1)S(1)}, bf16[1024,1024]{1,0:T(8,128)(2,1)}, u32[]{:S(2)}) copy-start(bf16[1024,1024]{1,0:T(8,128)(2,1)} %param.15) | copy-start | bytes 6291460
  33.5 60.9 %collective-permute-start.3 = (bf16[21,2,2,64,256]{4,3,2,1,0:T(8,128)(2,1)}, bf16[21,2,2,64,256]{4,3,2,1,0:T(8,128)(2,1)}, u32[]{:S(2)}, u32[]{:S(2)}) collective-permute-start(bf16[21,2,2,64,256]{4,3,2,1,0:T(8,128)(2,1)} %sums.7), channel_id=1, source_target_pairs={{0,16},{16,0},{1,17},{17,1},{2,18},{18,2},{3,19},{19,3},{4,20},{20... | collective-permute-start | bytes 8257544 | tf_op jit(solution)/shard_map/ppermute | solution.py:291
  100.4 7.7 %copy-start.7 = (f32[256]{0:T(256)S(1)}, f32[256]{0:T(256)}, u32[]{:S(2)}) copy-start(f32[256]{0:T(256)} %param.12) | copy-start | bytes 3076
  100.4 110.4 %all-to-all-start.6 = ((bf16[16,21,16,256]{3,2,1,0:T(8,128)(2,1)}), bf16[16,21,16,256]{3,2,1,0:T(8,128)(2,1)}, u32[]{:S(2)}, u32[]{:S(2)}) async-start(bf16[16,21,16,256]{3,2,1,0:T(8,128)(2,1)} %radial.7), calls=%async_computation.6 | async-start | bytes 5505024 | tf_op jit(solution)/shard_map/all_to_all | solution.py:311
  143.6 61.2 %collective-permute-start = (bf16[21,2,2,64,256]{4,3,2,1,0:T(8,128)(2,1)}, bf16[21,2,2,64,256]{4,3,2,1,0:T(8,128)(2,1)}, u32[]{:S(2)}, u32[]{:S(2)}) collective-permute-start(bf16[21,2,2,64,256]{4,3,2,1,0:T(8,128)(2,1)} %get-tuple-element.12), channel_id=1, source_target_pairs={{0,16},{16,0},{1,17},{17,1},{2,18},{18,2},{3,19},{19,3},{4,20},{20... | collective-permute-start | bytes 8257544 | tf_op jit(solution)/shard_map/ppermute | solution.py:291
  210.8 74.1 %all-to-all-start = ((bf16[16,21,16,256]{3,2,1,0:T(8,128)(2,1)}), bf16[16,21,16,256]{3,2,1,0:T(8,128)(2,1)}, u32[]{:S(2)}, u32[]{:S(2)}) async-start(bf16[16,21,16,256]{3,2,1,0:T(8,128)(2,1)} %radial.4), calls=%async_computation | async-start | bytes 5505024 | tf_op jit(solution)/shard_map/all_to_all | solution.py:311
  217.7 61.2 %collective-permute-start.1 = (bf16[21,2,2,64,256]{4,3,2,1,0:T(8,128)(2,1)}, bf16[21,2,2,64,256]{4,3,2,1,0:T(8,128)(2,1)}, u32[]{:S(2)}, u32[]{:S(2)}) collective-permute-start(bf16[21,2,2,64,256]{4,3,2,1,0:T(8,128)(2,1)} %get-tuple-element.14), channel_id=1, source_target_pairs={{0,16},{16,0},{1,17},{17,1},{2,18},{18,2},{3,19},{19,3},{4,20},{20... | collective-permute-start | bytes 8257544 | tf_op jit(solution)/shard_map/ppermute | solution.py:291
  284.9 74.2 %all-to-all-start.2 = ((bf16[16,21,16,256]{3,2,1,0:T(8,128)(2,1)}), bf16[16,21,16,256]{3,2,1,0:T(8,128)(2,1)}, u32[]{:S(2)}, u32[]{:S(2)}) async-start(bf16[16,21,16,256]{3,2,1,0:T(8,128)(2,1)} %radial.5), calls=%async_computation.2 | async-start | bytes 5505024 | tf_op jit(solution)/shard_map/all_to_all | solution.py:311
  291.8 61.2 %collective-permute-start.2 = (bf16[21,2,2,64,256]{4,3,2,1,0:T(8,128)(2,1)}, bf16[21,2,2,64,256]{4,3,2,1,0:T(8,128)(2,1)}, u32[]{:S(2)}, u32[]{:S(2)}) collective-permute-start(bf16[21,2,2,64,256]{4,3,2,1,0:T(8,128)(2,1)} %get-tuple-element.16), channel_id=1, source_target_pairs={{0,16},{16,0},{1,17},{17,1},{2,18},{18,2},{3,19},{19,3},{4,20},{20... | collective-permute-start | bytes 8257544 | tf_op jit(solution)/shard_map/ppermute | solution.py:291
  359.0 7.0 %copy-start.6 = (f32[84,256]{1,0:T(8,128)S(1)}, f32[84,256]{1,0:T(8,128)}, u32[]{:S(2)}) copy-start(f32[84,256]{1,0:T(8,128)} %param.14) | copy-start | bytes 258052
  359.0 68.6 %all-to-all-start.4 = ((bf16[16,21,16,256]{3,2,1,0:T(8,128)(2,1)}), bf16[16,21,16,256]{3,2,1,0:T(8,128)(2,1)}, u32[]{:S(2)}, u32[]{:S(2)}) async-start(bf16[16,21,16,256]{3,2,1,0:T(8,128)(2,1)} %radial.6), calls=%async_computation.4 | async-start | bytes 5505024 | tf_op jit(solution)/shard_map/all_to_all | solution.py:311
  366.9 4.1 copy-start.5
  427.6 36.7 %all-to-all-start.7 = ((bf16[16,21,16,128]{3,2,1,0:T(8,128)(2,1)}), bf16[16,21,16,128]{3,2,1,0:T(8,128)(2,1)S(1)}, u32[]{:S(2)}, u32[]{:S(2)}) async-start(bf16[16,21,16,128]{3,2,1,0:T(8,128)(2,1)} %axial.7), calls=%async_computation.7 | async-start | bytes 2752512 | tf_op jit(solution)/shard_map/all_to_all | solution.py:332
  464.4 1.1 copy-start.4
  465.5 36.7 %all-to-all-start.3 = ((bf16[16,21,16,128]{3,2,1,0:T(8,128)(2,1)}), bf16[16,21,16,128]{3,2,1,0:T(8,128)(2,1)S(1)}, u32[]{:S(2)}, u32[]{:S(2)}) async-start(bf16[16,21,16,128]{3,2,1,0:T(8,128)(2,1)} %axial.5), calls=%async_computation.3 | async-start | bytes 2752512 | tf_op jit(solution)/shard_map/all_to_all | solution.py:332
  502.2 15.1 %copy-start.2 = (bf16[16,21,16,128]{3,2,1,0:T(8,128)(2,1)}, bf16[16,21,16,128]{3,2,1,0:T(8,128)(2,1)S(1)}, u32[]{:S(2)}) copy-start(bf16[16,21,16,128]{3,2,1,0:T(8,128)(2,1)S(1)} %all-to-all-done.3.returned_ref) | copy-start | bytes 4128772
  502.2 36.7 %all-to-all-start.5 = ((bf16[16,21,16,128]{3,2,1,0:T(8,128)(2,1)}), bf16[16,21,16,128]{3,2,1,0:T(8,128)(2,1)S(1)}, u32[]{:S(2)}, u32[]{:S(2)}) async-start(bf16[16,21,16,128]{3,2,1,0:T(8,128)(2,1)} %axial.6), calls=%async_computation.5 | async-start | bytes 2752512 | tf_op jit(solution)/shard_map/all_to_all | solution.py:332
  538.9 9.9 %copy-start.3 = (bf16[16,21,16,128]{3,2,1,0:T(8,128)(2,1)}, bf16[16,21,16,128]{3,2,1,0:T(8,128)(2,1)S(1)}, u32[]{:S(2)}) copy-start(bf16[16,21,16,128]{3,2,1,0:T(8,128)(2,1)S(1)} %all-to-all-done.5.returned_ref) | copy-start | bytes 4128772
  538.9 36.8 %all-to-all-start.1 = ((bf16[16,21,16,128]{3,2,1,0:T(8,128)(2,1)}), bf16[16,21,16,128]{3,2,1,0:T(8,128)(2,1)}, u32[]{:S(2)}, u32[]{:S(2)}) async-start(bf16[16,21,16,128]{3,2,1,0:T(8,128)(2,1)} %axial.4), calls=%async_computation.1 | async-start | bytes 2752512 | tf_op jit(solution)/shard_map/all_to_all | solution.py:332
  575.7 5.3 copy-start.1
